TPU v7x, 32 devices: a whole 2x2x4 slice. The times are simulated.
32 devices in a mesh: strip: 8 (over y, x, core), mode: 4 (over z).
Axes of the slice: x: 2, y: 2, z: 4, core: 2. Of those that a mesh axis runs over, the one named last changes fastest.
Arguments:
- object_field: float32 [2, 2048, 384], P(None, 'strip'), may hold values from -5 to 5
- probe_modes: float32 [2, 8, 256, 256], P(None, 'mode'), may hold values from -2.5 to 2.5
- measured: float32 [8, 4, 256, 256], P('strip'), may hold values from 0.1 to 27
- positions: int32 [8, 4, 2], P('strip'), may hold values from 0 to 128, as said below
Outputs:
- object_new: float32 [2, 2048, 384], P(None, 'strip')
Inputs may be any that keep to these rules, and one draw needn't show every extreme that they name: positions[s,k,0] is the first row of window k within strip s and positions[s,k,1] its first column; the windows of every strip form a two by two raster with small offsets: windows 0 and 3 start at row 128, windows 1 and 2 at row 0, window 1 at column 128, window 3 at most 16 columns left of it, windows 0 and 2 at columns 0 to 16.
All inputs are finite; a program needn't handle non-finite values.
Results may differ from a plain program's by a relative error of at most 0.0001.
Values sent between devices are 32-bit elements; how exact they have to be, the bound alone decides.
A program may use at most 128 MiB of HBM per device.

v0:
```python
import jax
import jax.numpy as jnp
from jax import lax
from jax.sharding import PartitionSpec as P

HALO = 128
ITERS = 3
regularizer = 0.1
step_scale = 0.3
epsilon = 1e-06
highest = lax.Precision.HIGHEST


def from_behind(block, axis, distance):
    devices = range(lax.axis_size(axis))
    route = [(i - distance, i) for i in devices if i - distance in devices]
    return lax.ppermute(block, axis, route)


def dft_tables(length):
    indices = jnp.arange(length, dtype=jnp.int32)
    phases = indices[:, None] * indices[None, :] % length
    angles = phases.astype(jnp.float32) * (2.0 * jnp.pi / length)
    scaling = 1.0 / jnp.sqrt(jnp.float32(length))
    return (jnp.cos(angles) * scaling, -jnp.sin(angles) * scaling)


def transform(part_real, part_imag, cosine_table, sine_table):
    length = cosine_table.shape[0]
    stacked_rows = jnp.concatenate([cosine_table, sine_table], axis=0)
    left_real = jnp.einsum("jk,bkl->bjl", stacked_rows, part_real, precision=highest)
    left_imag = jnp.einsum("jk,bkl->bjl", stacked_rows, part_imag, precision=highest)
    middle_real = left_real[:, :length] - left_imag[:, length:]
    middle_imag = left_imag[:, :length] + left_real[:, length:]
    stacked_cols = jnp.concatenate([cosine_table, sine_table], axis=1)
    right_real = jnp.einsum("bjk,kl->bjl", middle_real, stacked_cols, precision=highest)
    right_imag = jnp.einsum("bjk,kl->bjl", middle_imag, stacked_cols, precision=highest)
    return (
        right_real[..., :length] - right_imag[..., length:],
        right_imag[..., :length] + right_real[..., length:],
    )


def body(object_field, probe_modes, measured, positions):
    stripe_rows = object_field.shape[1]
    width_cols = object_field.shape[2]
    window = probe_modes.shape[2]
    local_modes = probe_modes.shape[1]
    slots = positions.shape[1]
    halo_rows = HALO
    cosine_table, sine_table = dft_tables(window)
    rows_at = positions[0, :, 0]
    cols_at = positions[0, :, 1]
    total_cells = stripe_rows * lax.axis_size("strip") * width_cols
    measured_intensity = measured[0]
    probe_real = probe_modes[0][None]
    probe_imag = probe_modes[1][None]
    zero_index = jnp.zeros((), jnp.int32)
    for iteration in range(ITERS):
        below = from_behind(object_field[:, :halo_rows], "strip", -1)
        frame = jnp.concatenate([object_field, below], axis=1)
        patches = jnp.stack(
            [
                lax.dynamic_slice(
                    frame, (zero_index, rows_at[slot], cols_at[slot]), (2, window, window)
                )
                for slot in range(slots)
            ],
            axis=1,
        )
        patch_real = patches[0][:, None]
        patch_imag = patches[1][:, None]
        exit_real = probe_real * patch_real - probe_imag * patch_imag
        exit_imag = probe_real * patch_imag + probe_imag * patch_real
        far_real, far_imag = transform(
            exit_real.reshape(-1, window, window),
            exit_imag.reshape(-1, window, window),
            cosine_table,
            sine_table,
        )
        far_real = far_real.reshape(slots, local_modes, window, window)
        far_imag = far_imag.reshape(slots, local_modes, window, window)
        probe_power = jnp.sum(far_real * far_real + far_imag * far_imag, axis=1)
        summed_power = lax.psum(probe_power, "mode")
        object_update = (
            jnp.sqrt((measured_intensity + regularizer) / (summed_power + regularizer)) - 1.0
        )
        shift_real = (object_update[:, None] * far_real).reshape(-1, window, window)
        shift_imag = (object_update[:, None] * far_imag).reshape(-1, window, window)
        delta_real, delta_imag = transform(shift_real, shift_imag, cosine_table, -sine_table)
        delta_real = delta_real.reshape(slots, local_modes, window, window)
        delta_imag = delta_imag.reshape(slots, local_modes, window, window)
        grad_real = jnp.sum(probe_real * delta_real + probe_imag * delta_imag, axis=1)
        grad_imag = jnp.sum(probe_real * delta_imag - probe_imag * delta_real, axis=1)
        grad_real, grad_imag = lax.psum((grad_real, grad_imag), "mode")
        frame_grad = jnp.zeros((2, stripe_rows + halo_rows, width_cols), jnp.float32)
        for slot in range(slots):
            start = (zero_index, rows_at[slot], cols_at[slot])
            current = lax.dynamic_slice(frame_grad, start, (2, window, window))
            frame_grad = lax.dynamic_update_slice(
                frame_grad, current + jnp.stack([grad_real[slot], grad_imag[slot]]), start
            )
        arrived = from_behind(frame_grad[:, stripe_rows:], "strip", 1)
        gradient = jnp.concatenate(
            [frame_grad[:, :halo_rows] + arrived, frame_grad[:, halo_rows:stripe_rows]], axis=1
        )
        square_sum = lax.psum(jnp.sum(gradient * gradient), "strip")
        step_factor = step_scale / jnp.sqrt(square_sum / total_cells + epsilon)
        object_field = object_field + step_factor * gradient
    return object_field


def solution(mesh):
    return jax.shard_map(
        body,
        mesh=mesh,
        in_specs=(
            P(None, "strip", None),
            P(None, "mode", None, None),
            P("strip", None, None, None),
            P("strip", None, None),
        ),
        out_specs=P(None, "strip", None),
        check_vma=False,
    )
```

profile of v0, /device:TPU:4, one launch (start us, length us, event | category | flops | bytes accessed | tf_op | source)
XLA Modules:
  0.0 812.3 jit_solution(13496103538297187486)
XLA Ops:
  8.4 2.8 collective-permute-start
  31.6 7.1 convolution_bitcast_fusion.10
  38.7 7.5 convolution_bitcast_fusion.11
  46.3 3.7 fusion.22
  50.0 3.7 fusion.20
  53.7 1.9 copy-done.1
  58.5 51.5 %all-reduce.10.cloned.1.call-done = f32[4,256,256]{2,1,0:T(8,128)} async-done(((f32[4,256,256]{2,1,0:T(8,128)}), f32[4,256,256]{2,1,0:T(8,128)}) %all-reduce.10.cloned.1.call-update) | async-done | bytes 1048592 | tf_op jit(solution)/shard_map/psum | solution.py:84
  111.6 4.1 bitcast_multiply_fusion.5
  115.7 7.2 convolution_bitcast_fusion.9
  122.9 7.6 convolution_bitcast_fusion.8
  130.5 3.7 fusion.16
  134.2 3.7 fusion.18
  137.9 2.1 add_reduce_fusion.2
  140.1 85.5 %all-reduce.20.cloned.1.call-done = (f32[4,256,256]{2,1,0:T(8,128)}, f32[4,256,256]{2,1,0:T(8,128)}) async-done(((f32[4,256,256]{2,1,0:T(8,128)}, f32[4,256,256]{2,1,0:T(8,128)}), (f32[4,256,256]{2,1,0:T(8,128)}, f32[4,256,256]{2,1,0:T(8,128)})) %all-reduce.20.cloned.1.call-update) | async-done | bytes 2097168 | tf_op jit(solution)/shard_map/psum | solution.py:95
  225.6 2.2 fusion.109
  228.8 6.6 dynamic_update_slice.36
  236.6 5.3 dynamic_update_slice.37
  243.2 8.1 dynamic_update_slice.38
  252.5 6.6 dynamic_update_slice.39
  261.1 8.1 collective-permute-done.1
  270.8 12.5 %psum.87 = f32[]{:T(128)} all-reduce(f32[]{:T(128)} %multiply_reduce_fusion.2), channel_id=1, replica_groups=mesh['strip'=8,'mode'=4] {'strip'}, use_global_device_ids=true, to_apply=%region_7.8 | all-reduce | flops 1 | bytes 8 | tf_op jit(solution)/shard_map/psum | solution.py:107
  285.3 2.1 collective-permute-start.2
  287.4 5.1 collective-permute-done.2
  294.6 7.1 convolution_bitcast_fusion.6
  301.7 7.3 convolution_bitcast_fusion.7
  309.0 3.7 fusion.14
  312.8 3.7 fusion.12
  320.6 51.1 %all-reduce.12.cloned.1.call-done = f32[4,256,256]{2,1,0:T(8,128)} async-done(((f32[4,256,256]{2,1,0:T(8,128)}), f32[4,256,256]{2,1,0:T(8,128)}) %all-reduce.12.cloned.1.call-update) | async-done | bytes 1048592 | tf_op jit(solution)/shard_map/psum | solution.py:84
  373.3 4.1 bitcast_multiply_fusion.3
  377.4 7.2 convolution_bitcast_fusion.5
  384.6 7.4 convolution_bitcast_fusion.4
  391.9 3.7 fusion.8
  395.6 3.7 fusion.10
  399.3 2.1 add_reduce_fusion.1
  401.5 85.5 %all-reduce.18.cloned.1.call-done = (f32[4,256,256]{2,1,0:T(8,128)}, f32[4,256,256]{2,1,0:T(8,128)}) async-done(((f32[4,256,256]{2,1,0:T(8,128)}, f32[4,256,256]{2,1,0:T(8,128)}), (f32[4,256,256]{2,1,0:T(8,128)}, f32[4,256,256]{2,1,0:T(8,128)})) %all-reduce.18.cloned.1.call-update) | async-done | bytes 2097168 | tf_op jit(solution)/shard_map/psum | solution.py:95
  487.0 2.2 fusion.107
  490.2 6.6 dynamic_update_slice.40
  498.0 5.3 dynamic_update_slice.41
  504.6 8.1 dynamic_update_slice.42
  513.9 6.6 dynamic_update_slice.43
  522.5 8.1 collective-permute-done.3
  532.2 12.5 %psum.91 = f32[]{:T(128)} all-reduce(f32[]{:T(128)} %multiply_reduce_fusion.1), channel_id=1, replica_groups=mesh['strip'=8,'mode'=4] {'strip'}, use_global_device_ids=true, to_apply=%region_15.16 | all-reduce | flops 1 | bytes 8 | tf_op jit(solution)/shard_map/psum | solution.py:107
  546.8 2.3 collective-permute-start.4
  549.1 4.9 collective-permute-done.4
  556.1 7.1 convolution_bitcast_fusion.2
  563.1 7.2 convolution_bitcast_fusion.3
  570.4 3.7 fusion.6
  574.1 3.7 fusion.4
  581.7 51.3 %all-reduce.14.cloned.1.call-done = f32[4,256,256]{2,1,0:T(8,128)} async-done(((f32[4,256,256]{2,1,0:T(8,128)}), f32[4,256,256]{2,1,0:T(8,128)}) %all-reduce.14.cloned.1.call-update) | async-done | bytes 1048592 | tf_op jit(solution)/shard_map/psum | solution.py:84
  633.0 2.0 fusion.29
  634.9 4.1 bitcast_multiply_fusion.1
  639.0 7.2 convolution_bitcast_fusion.1
  646.2 7.6 convolution_bitcast_fusion
  653.8 3.7 fusion
  657.5 3.7 fusion.2
  661.2 2.1 add_reduce_fusion
  663.3 85.6 %all-reduce.16.cloned.1.call-done = (f32[4,256,256]{2,1,0:T(8,128)}, f32[4,256,256]{2,1,0:T(8,128)}) async-done(((f32[4,256,256]{2,1,0:T(8,128)}, f32[4,256,256]{2,1,0:T(8,128)}), (f32[4,256,256]{2,1,0:T(8,128)}, f32[4,256,256]{2,1,0:T(8,128)})) %all-reduce.16.cloned.1.call-update) | async-done | bytes 2097168 | tf_op jit(solution)/shard_map/psum | solution.py:95
  748.9 2.1 fusion.105
  751.9 6.8 dynamic_update_slice.44
  759.9 5.3 dynamic_update_slice.45
  765.4 8.1 dynamic_update_slice.46
  773.7 6.6 dynamic_update_slice.47
  782.2 8.1 collective-permute-done.5
  791.2 12.5 %psum.95 = f32[]{:T(128)} all-reduce(f32[]{:T(128)} %multiply_reduce_fusion), channel_id=1, replica_groups=mesh['strip'=8,'mode'=4] {'strip'}, use_global_device_ids=true, to_apply=%region_23.24 | all-reduce | flops 1 | bytes 8 | tf_op jit(solution)/shard_map/psum | solution.py:107
  (101 shorter events, 51.2 us)
Async XLA Ops:
  6.5 23.4 %copy-start.11 = (f32[2,2,256,256]{3,2,1,0:T(8,128)S(1)}, f32[2,2,256,256]{3,2,1,0:T(8,128)}, u32[]{:S(2)}) copy-start(f32[2,2,256,256]{3,2,1,0:T(8,128)} %param.5) | copy-start | bytes 3145732
  6.5 103.5 %all-reduce.10.cloned.1.call-start = ((), (), s32[]{:S(2)}) async-start(), calls=%async_computation | async-start | bytes 2097152 | tf_op jit(solution)/shard_map/psum | solution.py:84
  8.4 21.7 %collective-permute-start = (f32[2,128,384]{2,1,0:T(8,128)}, f32[2,128,384]{2,1,0:T(8,128)S(1)}, u32[]{:S(2)}, u32[]{:S(2)}) collective-permute-start(f32[2,128,384]{2,1,0:T(8,128)} %slice.359), channel_id=1, source_target_pairs={{4,0},{8,4},{12,8},{16,12},{20,16},{24,20},{28,24},{5,1},{9,5},{13... | collective-permute-start | bytes 1179656 | tf_op jit(solution)/shard_map/ppermute | solution.py:17
  50.0 3.7 copy-start
  53.7 1.9 copy-start.1
  55.7 54.3 %copy-start.7 = (f32[1,4,256,256]{3,2,1,0:T(8,128)S(1)}, f32[1,4,256,256]{3,2,1,0:T(8,128)}, u32[]{:S(2)}) copy-start(f32[1,4,256,256]{3,2,1,0:T(8,128)} %param.6) | copy-start | bytes 3145732
  57.4 168.2 %all-reduce.20.cloned.1.call-start = ((), (), s32[]{:S(2)}) async-start(), calls=%async_computation.5 | async-start | bytes 4194304 | tf_op jit(solution)/shard_map/psum | solution.py:95
  140.0 231.6 %all-reduce.12.cloned.1.call-start = ((), (), s32[]{:S(2)}) async-start(), calls=%async_computation.1 | async-start | bytes 2097152 | tf_op jit(solution)/shard_map/psum | solution.py:84
  225.6 2.2 copy-start.12
  259.1 10.0 %collective-permute-start.1 = (f32[2,128,384]{2,1,0:T(8,128)S(1)}, f32[2,128,384]{2,1,0:T(8,128)S(1)}, u32[]{:S(2)}, u32[]{:S(2)}) collective-permute-start(f32[2,128,384]{2,1,0:T(8,128)S(1)} %slice.485), channel_id=1, source_target_pairs={{0,4},{4,8},{8,12},{12,16},{16,20},{20,24},{24,28},{1,5},{5,9},{9,... | collective-permute-start | bytes 1179656 | tf_op jit(solution)/shard_map/ppermute | solution.py:17
  269.2 0.7 copy-start.10
  285.3 8.6 %copy-start.6 = (f32[2,256,384]{2,1,0:T(8,128)}, f32[2,256,384]{2,1,0:T(8,128)S(1)}, u32[]{:S(2)}) copy-start(f32[2,256,384]{2,1,0:T(8,128)S(1)} %multiply_add_fusion.8) | copy-start | bytes 2359300
  285.3 7.2 collective-permute-start.2
  312.7 3.7 copy-start.4
  316.5 1.9 copy-start.5
  318.4 53.2 %copy-start.8 = (f32[1,4,256,256]{3,2,1,0:T(8,128)S(1)}, f32[1,4,256,256]{3,2,1,0:T(8,128)}, u32[]{:S(2)}) copy-start(f32[1,4,256,256]{3,2,1,0:T(8,128)} %param.6) | copy-start | bytes 3145732
  320.0 167.0 %all-reduce.18.cloned.1.call-start = ((), (), s32[]{:S(2)}) async-start(), calls=%async_computation.4 | async-start | bytes 4194304 | tf_op jit(solution)/shard_map/psum | solution.py:95
  401.4 231.6 %all-reduce.14.cloned.1.call-start = ((), (), s32[]{:S(2)}) async-start(), calls=%async_computation.2 | async-start | bytes 2097152 | tf_op jit(solution)/shard_map/psum | solution.py:84
  487.0 2.2 copy-start.13
  520.5 10.0 %collective-permute-start.3 = (f32[2,128,384]{2,1,0:T(8,128)S(1)}, f32[2,128,384]{2,1,0:T(8,128)S(1)}, u32[]{:S(2)}, u32[]{:S(2)}) collective-permute-start(f32[2,128,384]{2,1,0:T(8,128)S(1)} %slice.515), channel_id=1, source_target_pairs={{0,4},{4,8},{8,12},{12,16},{16,20},{20,24},{24,28},{1,5},{5,9},{9,... | collective-permute-start | bytes 1179656 | tf_op jit(solution)/shard_map/ppermute | solution.py:17
  530.6 0.7 copy-start.9
  546.8 7.2 collective-permute-start.4
  574.1 3.7 copy-start.2
  577.8 1.9 copy-start.3
  581.4 167.5 %all-reduce.16.cloned.1.call-start = ((), (), s32[]{:S(2)}) async-start(), calls=%async_computation.3 | async-start | bytes 4194304 | tf_op jit(solution)/shard_map/psum | solution.py:95
  748.9 2.1 copy-start.14
  780.3 10.0 %collective-permute-start.5 = (f32[2,128,384]{2,1,0:T(8,128)S(1)}, f32[2,128,384]{2,1,0:T(8,128)S(1)}, u32[]{:S(2)}, u32[]{:S(2)}) collective-permute-start(f32[2,128,384]{2,1,0:T(8,128)S(1)} %slice.545), channel_id=1, source_target_pairs={{0,4},{4,8},{8,12},{12,16},{16,20},{20,24},{24,28},{1,5},{5,9},{9,... | collective-permute-start | bytes 1179656 | tf_op jit(solution)/shard_map/ppermute | solution.py:17
Sparse Core Ops, SparseCore 0:
  57.6 52.3 all-reduce.9
  140.1 85.4 all-reduce.19
  320.2 51.4 all-reduce.11
  401.5 85.4 all-reduce.17
  581.5 51.4 all-reduce.13
  663.4 85.4 all-reduce.15
where the time goes:
time: 822 us; the launch traced here: 812 us
  waiting for transfers between devices  445 us (54%)
  matrix products  132 us (16%)
  local copies, waits for them, and re-layouts  102 us (12%)
  other arithmetic  50.7 us (6%)
  blocking collectives  37.5 us (5%)
  between operations  31.3 us (4%)
  starting transfers between devices  13.8 us (2%)
    psum x3, waiting for transfers between devices, body(): grad_real, grad_imag = lax.psum((grad_real, grad_imag), 'mode')  257 us
    psum x3, waiting for transfers between devices, body(): summed_power = lax.psum(probe_power, 'mode')  154 us
    dynamic_update_slice x12, local copies, waits for them, and re-layouts, body(): lax.dynamic_update_slice(frame_grad, current + jnp.stack([grad_real[slot]...  79.7 us
    dot_general x6, matrix products, transform(): jnp.einsum('jk,bkl->bjl', stacked_rows, part_imag, precision=highest)  43.8 us
    dot_general x6, matrix products, transform(): jnp.einsum('jk,bkl->bjl', stacked_rows, part_real, precision=highest)  43.7 us
    psum x3, blocking collectives, body(): square_sum = lax.psum(jnp.sum(gradient * gradient), 'strip')  37.5 us
    ppermute x6, waiting for transfers between devices, from_behind(): return lax.ppermute(block, axis, route)  34.2 us
    dot_general x6, matrix products, transform(): jnp.einsum('bjk,kl->bjl', middle_real, stacked_cols, precision=highest)  22.2 us
  transfers between devices with their start and end apart: 12, of which 11 were waited for; matrix products, arithmetic and copies ran while one was open for 1% of the time, Pallas kernels for 0%

commit v1 on v0

--- a/solution.py
+++ b/solution.py
@@ -81,7 +81,8 @@
         far_real = far_real.reshape(slots, local_modes, window, window)
         far_imag = far_imag.reshape(slots, local_modes, window, window)
         probe_power = jnp.sum(far_real * far_real + far_imag * far_imag, axis=1)
-        summed_power = lax.psum(probe_power, "mode")
+        pieces = lax.all_gather(probe_power, "mode")
+        summed_power = jnp.sum(pieces, axis=0)
         object_update = (
             jnp.sqrt((measured_intensity + regularizer) / (summed_power + regularizer)) - 1.0
         )

time: 822 us -> 918 us (1.12)
  waiting for transfers between devices: 445 us -> 529 us
  other arithmetic: 50.7 us -> 63.3 us
    all_gather x0 -> x3, waiting for transfers between devices: none -> 240 us  [body(): pieces = lax.all_gather(probe_power, 'mode')]
    psum x3 -> x0, waiting for transfers between devices: 154 us -> none  [body(): summed_power = lax.psum(probe_power, 'mode')]
    reduce_sum x0 -> x3, other arithmetic: none -> 11.1 us  [body(): summed_power = jnp.sum(pieces, axis=0)]
where the time goes in v1:
time: 918 us; the launch traced here: 909 us
  waiting for transfers between devices  529 us (58%)
  matrix products  131 us (14%)
  local copies, waits for them, and re-layouts  102 us (11%)
  other arithmetic  63.3 us (7%)
  blocking collectives  37.5 us (4%)
  between operations  31.3 us (3%)
  starting transfers between devices  13.6 us (1%)
    psum x3, waiting for transfers between devices, body(): grad_real, grad_imag = lax.psum((grad_real, grad_imag), 'mode')  254 us
    all_gather x3, waiting for transfers between devices, body(): pieces = lax.all_gather(probe_power, 'mode')  240 us
    dynamic_update_slice x12, local copies, waits for them, and re-layouts, body(): lax.dynamic_update_slice(frame_grad, current + jnp.stack([grad_real[slot]...  79.7 us
    dot_general x6, matrix products, transform(): jnp.einsum('jk,bkl->bjl', stacked_rows, part_imag, precision=highest)  43.6 us
    dot_general x6, matrix products, transform(): jnp.einsum('jk,bkl->bjl', stacked_rows, part_real, precision=highest)  43.4 us
    psum x3, blocking collectives, body(): square_sum = lax.psum(jnp.sum(gradient * gradient), 'strip')  37.5 us
    ppermute x6, waiting for transfers between devices, from_behind(): return lax.ppermute(block, axis, route)  34.3 us
    dot_general x6, matrix products, transform(): jnp.einsum('bjk,kl->bjl', middle_imag, stacked_cols, precision=highest)  22.2 us
  transfers between devices with their start and end apart: 12, of which 11 were waited for; matrix products, arithmetic and copies ran while one was open for 1% of the time, Pallas kernels for 0%

profile of v1, /device:TPU:4, one launch (start us, length us, event | category | flops | bytes accessed | tf_op | source)
XLA Modules:
  0.0 908.6 jit_solution(3797961129989030444)
XLA Ops:
  8.4 2.8 collective-permute-start
  31.6 7.1 convolution_bitcast_fusion.10
  38.7 7.3 convolution_bitcast_fusion.11
  46.0 3.7 fusion.22
  49.7 3.7 fusion.20
  58.5 80.4 %all-gather.7.cloned.1.call-done = f32[16,256,256]{2,1,0:T(8,128)} async-done(((f32[4,256,256]{2,1,0:T(8,128)}), f32[16,256,256]{2,1,0:T(8,128)}) %all-gather.7.cloned.1.call-update) | async-done | bytes 4194320 | tf_op jit(solution)/shard_map/all_gather | solution.py:84
  138.9 3.7 reduce_sum.136
  144.2 4.1 bitcast_multiply_fusion.5
  148.3 7.2 convolution_bitcast_fusion.9
  155.5 7.4 convolution_bitcast_fusion.8
  162.9 3.7 fusion.16
  166.6 3.7 fusion.18
  170.3 2.2 add_reduce_fusion.2
  172.5 84.8 %all-reduce.11.cloned.1.call-done = (f32[4,256,256]{2,1,0:T(8,128)}, f32[4,256,256]{2,1,0:T(8,128)}) async-done(((f32[4,256,256]{2,1,0:T(8,128)}, f32[4,256,256]{2,1,0:T(8,128)}), (f32[4,256,256]{2,1,0:T(8,128)}, f32[4,256,256]{2,1,0:T(8,128)})) %all-reduce.11.cloned.1.call-update) | async-done | bytes 2097168 | tf_op jit(solution)/shard_map/psum | solution.py:96
  257.3 2.2 fusion.109
  260.5 6.6 dynamic_update_slice.36
  268.3 5.3 dynamic_update_slice.37
  274.9 8.1 dynamic_update_slice.38
  284.2 6.6 dynamic_update_slice.39
  292.8 8.1 collective-permute-done.1
  302.5 12.5 %psum.65 = f32[]{:T(128)} all-reduce(f32[]{:T(128)} %multiply_reduce_fusion.2), channel_id=1, replica_groups=mesh['strip'=8,'mode'=4] {'strip'}, use_global_device_ids=true, to_apply=%region_7.8 | all-reduce | flops 1 | bytes 8 | tf_op jit(solution)/shard_map/psum | solution.py:108
  319.0 5.3 collective-permute-done.2
  326.3 7.1 convolution_bitcast_fusion.6
  333.4 7.3 convolution_bitcast_fusion.7
  340.7 3.7 fusion.14
  344.4 3.7 fusion.12
  352.2 80.0 %all-gather.9.cloned.1.call-done = f32[16,256,256]{2,1,0:T(8,128)} async-done(((f32[4,256,256]{2,1,0:T(8,128)}), f32[16,256,256]{2,1,0:T(8,128)}) %all-gather.9.cloned.1.call-update) | async-done | bytes 4194320 | tf_op jit(solution)/shard_map/all_gather | solution.py:84
  432.2 3.7 reduce_sum.141
  437.5 4.1 bitcast_multiply_fusion.3
  441.6 7.2 convolution_bitcast_fusion.5
  448.8 7.4 convolution_bitcast_fusion.4
  456.2 3.7 fusion.8
  459.9 3.7 fusion.10
  463.6 2.1 add_reduce_fusion.1
  465.7 84.8 %all-reduce.9.cloned.1.call-done = (f32[4,256,256]{2,1,0:T(8,128)}, f32[4,256,256]{2,1,0:T(8,128)}) async-done(((f32[4,256,256]{2,1,0:T(8,128)}, f32[4,256,256]{2,1,0:T(8,128)}), (f32[4,256,256]{2,1,0:T(8,128)}, f32[4,256,256]{2,1,0:T(8,128)})) %all-reduce.9.cloned.1.call-update) | async-done | bytes 2097168 | tf_op jit(solution)/shard_map/psum | solution.py:96
  550.5 2.2 fusion.107
  553.7 6.6 dynamic_update_slice.40
  561.5 5.3 dynamic_update_slice.41
  568.1 8.1 dynamic_update_slice.42
  577.4 6.6 dynamic_update_slice.43
  586.0 8.1 collective-permute-done.3
  595.7 12.5 %psum.68 = f32[]{:T(128)} all-reduce(f32[]{:T(128)} %multiply_reduce_fusion.1), channel_id=1, replica_groups=mesh['strip'=8,'mode'=4] {'strip'}, use_global_device_ids=true, to_apply=%region_15.16 | all-reduce | flops 1 | bytes 8 | tf_op jit(solution)/shard_map/psum | solution.py:108
  610.3 2.3 collective-permute-start.4
  612.6 4.9 collective-permute-done.4
  619.5 7.1 convolution_bitcast_fusion.2
  626.6 7.2 convolution_bitcast_fusion.3
  633.9 3.7 fusion.6
  637.6 3.7 fusion.4
  645.2 80.2 %all-gather.11.cloned.1.call-done = f32[16,256,256]{2,1,0:T(8,128)} async-done(((f32[4,256,256]{2,1,0:T(8,128)}), f32[16,256,256]{2,1,0:T(8,128)}) %all-gather.11.cloned.1.call-update) | async-done | bytes 4194320 | tf_op jit(solution)/shard_map/all_gather | solution.py:84
  725.4 3.6 reduce_sum.146
  731.0 4.1 bitcast_multiply_fusion.1
  735.1 7.2 convolution_bitcast_fusion.1
  742.3 7.6 convolution_bitcast_fusion
  749.9 3.7 fusion
  753.6 3.7 fusion.2
  757.3 2.1 add_reduce_fusion
  759.4 84.8 %all-reduce.7.cloned.1.call-done = (f32[4,256,256]{2,1,0:T(8,128)}, f32[4,256,256]{2,1,0:T(8,128)}) async-done(((f32[4,256,256]{2,1,0:T(8,128)}, f32[4,256,256]{2,1,0:T(8,128)}), (f32[4,256,256]{2,1,0:T(8,128)}, f32[4,256,256]{2,1,0:T(8,128)})) %all-reduce.7.cloned.1.call-update) | async-done | bytes 2097168 | tf_op jit(solution)/shard_map/psum | solution.py:96
  844.2 2.1 fusion.105
  847.2 6.8 dynamic_update_slice.44
  855.2 5.3 dynamic_update_slice.45
  861.7 8.1 dynamic_update_slice.46
  870.0 6.6 dynamic_update_slice.47
  878.5 8.1 collective-permute-done.5
  887.5 12.5 %psum.71 = f32[]{:T(128)} all-reduce(f32[]{:T(128)} %multiply_reduce_fusion), channel_id=1, replica_groups=mesh['strip'=8,'mode'=4] {'strip'}, use_global_device_ids=true, to_apply=%region_23.24 | all-reduce | flops 1 | bytes 8 | tf_op jit(solution)/shard_map/psum | solution.py:108
  (104 shorter events, 58.4 us)
Async XLA Ops:
  6.5 23.4 %copy-start.11 = (f32[2,2,256,256]{3,2,1,0:T(8,128)S(1)}, f32[2,2,256,256]{3,2,1,0:T(8,128)}, u32[]{:S(2)}) copy-start(f32[2,2,256,256]{3,2,1,0:T(8,128)} %param.5) | copy-start | bytes 3145732
  6.5 132.3 %all-gather.7.cloned.1.call-start = ((), (), s32[]{:S(2)}) async-start(), calls=%async_computation | async-start | bytes 5242880 | tf_op jit(solution)/shard_map/all_gather | solution.py:84
  8.4 21.7 %collective-permute-start = (f32[2,128,384]{2,1,0:T(8,128)}, f32[2,128,384]{2,1,0:T(8,128)S(1)}, u32[]{:S(2)}, u32[]{:S(2)}) collective-permute-start(f32[2,128,384]{2,1,0:T(8,128)} %slice.359), channel_id=1, source_target_pairs={{4,0},{8,4},{12,8},{16,12},{20,16},{24,20},{28,24},{5,1},{9,5},{13... | collective-permute-start | bytes 1179656 | tf_op jit(solution)/shard_map/ppermute | solution.py:17
  49.7 3.7 copy-start
  53.4 1.9 copy-start.1
  57.5 199.9 %all-reduce.11.cloned.1.call-start = ((), (), s32[]{:S(2)}) async-start(), calls=%async_computation.5 | async-start | bytes 4194304 | tf_op jit(solution)/shard_map/psum | solution.py:96
  138.9 3.7 copy-start.7
  172.5 259.7 %all-gather.9.cloned.1.call-start = ((), (), s32[]{:S(2)}) async-start(), calls=%async_computation.1 | async-start | bytes 5242880 | tf_op jit(solution)/shard_map/all_gather | solution.py:84
  257.3 2.2 copy-start.12
  290.8 10.0 %collective-permute-start.1 = (f32[2,128,384]{2,1,0:T(8,128)S(1)}, f32[2,128,384]{2,1,0:T(8,128)S(1)}, u32[]{:S(2)}, u32[]{:S(2)}) collective-permute-start(f32[2,128,384]{2,1,0:T(8,128)S(1)} %slice.485), channel_id=1, source_target_pairs={{0,4},{4,8},{8,12},{12,16},{16,20},{20,24},{24,28},{1,5},{5,9},{9,... | collective-permute-start | bytes 1179656 | tf_op jit(solution)/shard_map/ppermute | solution.py:17
  300.9 0.7 copy-start.10
  317.0 8.6 copy-start.6
  317.0 7.2 collective-permute-start.2
  344.4 3.7 copy-start.4
  348.1 1.9 copy-start.5
  351.8 198.7 %all-reduce.9.cloned.1.call-start = ((), (), s32[]{:S(2)}) async-start(), calls=%async_computation.4 | async-start | bytes 4194304 | tf_op jit(solution)/shard_map/psum | solution.py:96
  432.2 3.7 copy-start.8
  465.7 259.7 %all-gather.11.cloned.1.call-start = ((), (), s32[]{:S(2)}) async-start(), calls=%async_computation.2 | async-start | bytes 5242880 | tf_op jit(solution)/shard_map/all_gather | solution.py:84
  550.5 2.2 copy-start.13
  584.0 10.0 %collective-permute-start.3 = (f32[2,128,384]{2,1,0:T(8,128)S(1)}, f32[2,128,384]{2,1,0:T(8,128)S(1)}, u32[]{:S(2)}, u32[]{:S(2)}) collective-permute-start(f32[2,128,384]{2,1,0:T(8,128)S(1)} %slice.515), channel_id=1, source_target_pairs={{0,4},{4,8},{8,12},{12,16},{16,20},{20,24},{24,28},{1,5},{5,9},{9,... | collective-permute-start | bytes 1179656 | tf_op jit(solution)/shard_map/ppermute | solution.py:17
  594.1 0.7 copy-start.9
  610.3 7.2 collective-permute-start.4
  637.6 3.7 copy-start.2
  641.4 1.9 copy-start.3
  645.0 199.2 %all-reduce.7.cloned.1.call-start = ((), (), s32[]{:S(2)}) async-start(), calls=%async_computation.3 | async-start | bytes 4194304 | tf_op jit(solution)/shard_map/psum | solution.py:96
  844.2 2.1 copy-start.14
  876.6 10.0 %collective-permute-start.5 = (f32[2,128,384]{2,1,0:T(8,128)S(1)}, f32[2,128,384]{2,1,0:T(8,128)S(1)}, u32[]{:S(2)}, u32[]{:S(2)}) collective-permute-start(f32[2,128,384]{2,1,0:T(8,128)S(1)} %slice.545), channel_id=1, source_target_pairs={{0,4},{4,8},{8,12},{12,16},{16,20},{20,24},{24,28},{1,5},{5,9},{9,... | collective-permute-start | bytes 1179656 | tf_op jit(solution)/shard_map/ppermute | solution.py:17
Sparse Core Ops, SparseCore 0:
  57.6 81.2 all-gather.6
  172.6 84.6 all-reduce.10
  351.9 80.2 all-gather.8
  465.8 84.6 all-reduce.8
  645.1 80.2 all-gather.10
  759.5 84.6 all-reduce.6
